TPU v7x, 32 devices: a whole 2x2x4 slice. The times are simulated.
32 devices in a mesh: tm: 16 (over z, y, x), col: 2 (over core).
Axes of the slice: x: 2, y: 2, z: 4, core: 2. Of those that a mesh axis runs over, the one named last changes fastest.
Arguments:
- diagonal_blocks: float32 [32, 512, 512], P('tm', 'col'), as said below
- upper_blocks: float32 [32, 512, 512], P('tm', 'col')
- right_sides: float32 [32, 512, 512], P('tm', 'col'), may hold values from -6 to 6
Outputs:
- reduced_blocks: float32 [32, 512, 512], P('tm', 'col')
- reduced_uppers: float32 [32, 512, 512], P('tm', 'col')
- reduced_sources: float32 [32, 512, 512], P('tm', 'col')
Inputs may be any that keep to these rules, and one draw needn't show every extreme that they name: `diagonal_blocks`: every block is symmetric, and the block-tridiagonal matrix built from these blocks and upper_blocks is positive definite.
All inputs are finite; a program needn't handle non-finite values.
Results may differ from a plain program's by a relative error of at most 0.0001.
Values sent between devices are 32-bit elements; how exact they have to be, the bound alone decides.
A program may use at most 64 MiB of HBM per device.

v0:
```python
import functools

import jax
import jax.numpy as jnp
from jax import lax
from jax.experimental import pallas as pl
from jax.experimental.pallas import tpu as pltpu
from jax.sharding import PartitionSpec as P

LEVELS = 2
TILE = 128
PANEL = 8
F32 = jnp.float32
BF16 = jnp.bfloat16


def split(values):
    high = values.astype(BF16)
    return high, (values - high.astype(F32)).astype(BF16)


def dot_parts(left, right, dims):
    def one(a, b):
        return lax.dot_general(a, b, (dims, ((), ())), preferred_element_type=F32)

    return one(left[0], right[0]) + (one(left[0], right[1]) + one(left[1], right[0]))


def dot3(left, right, dims=((1,), (0,))):
    return dot_parts(split(left), split(right), dims)


def panel_step(a, p):
    size = a[0].shape[1]
    count = size // PANEL
    base = PANEL * p
    lanes = lax.broadcasted_iota(jnp.int32, (PANEL, size), 1)
    subs = lax.broadcasted_iota(jnp.int32, (PANEL, size), 0)
    inside = jnp.logical_and(lanes >= base, lanes < base + PANEL)

    def spread(values, i):
        return jnp.broadcast_to(values[:, base + i : base + i + 1], (PANEL, size))

    head = [spread(a[p], i) for i in range(PANEL)]
    s = [
        [jnp.broadcast_to(head[j][i : i + 1, :], (PANEL, size)) if j >= i else None for j in range(PANEL)]
        for i in range(PANEL)
    ]
    rows = [
        jnp.where(
            inside,
            jnp.where(lanes == base + i, 1.0, 0.0),
            jnp.broadcast_to(a[p][i : i + 1, :], (PANEL, size)),
        )
        for i in range(PANEL)
    ]
    scale = [None] * PANEL
    low = {}
    for k in range(PANEL):
        scale[k] = 1.0 / s[k][k]
        for i in range(k + 1, PANEL):
            low[i, k] = s[k][i] * scale[k]
            for j in range(i, PANEL):
                s[i][j] = s[i][j] - low[i, k] * s[k][j]
            rows[i] = rows[i] - low[i, k] * rows[k]
    for k in range(PANEL):
        rows[k] = rows[k] * scale[k]
    for k in range(PANEL - 1, 0, -1):
        for i in range(k):
            rows[i] = rows[i] - low[k, i] * rows[k]
    solved = rows[0]
    for i in range(1, PANEL):
        solved = jnp.where(subs == i, rows[i], solved)
    fresh = [None] * count
    fresh[p] = solved
    for step in range(1, count):
        g = (p + step) % count
        col = [spread(a[g], i) for i in range(PANEL)]
        terms = [col[i] * rows[i] for i in range(PANEL)]
        while len(terms) > 1:
            terms = [terms[i] + terms[i + 1] for i in range(0, len(terms), 2)]
        fresh[g] = jnp.where(inside, 0.0, a[g]) - terms[0]
    return fresh


INNER = ((1,), (0,))
OUTER = ((1,), (1,))
CHUNKS = 4


def invert(s_ref, tile_ref):
    size = s_ref.shape[0]
    blocks = size // TILE

    @pl.loop(0, blocks)
    def _(k):
        at = pl.ds(pl.multiple_of(k * TILE, TILE), TILE)
        groups = [
            s_ref[pl.ds(pl.multiple_of(k * TILE, TILE) + PANEL * g, PANEL), at]
            for g in range(TILE // PANEL)
        ]
        for p in range(TILE // PANEL):
            groups = panel_step(groups, p)
        for g in range(TILE // PANEL):
            tile_ref[PANEL * g : PANEL * (g + 1), :] = groups[g]
        inverse = tile_ref[...]
        row = dot3(inverse, s_ref[at, :])
        s_ref[at, :] = row
        s_ref[at, at] = inverse
        row_parts = split(s_ref[at, :])
        for r in range(blocks):

            @pl.when(r != k)
            def _():
                rat = slice(r * TILE, (r + 1) * TILE)
                column = s_ref[rat, at]
                s_ref[rat, at] = jnp.zeros((TILE, TILE), F32)
                s_ref[rat, :] = s_ref[rat, :] - dot_parts(split(column), row_parts, INNER)


def kernel(
    tm_size, d_ref, u_ref, f_ref, dout_ref, uout_ref, fout_ref,
    s_ref, tile_ref, z_ref, full_ref, zown, cur, bufs, send_sem, recv_sem,
):
    half, size = d_ref.shape[1], d_ref.shape[2]
    column = lax.axis_index("col")
    place = lax.axis_index("tm")
    above, below = lax.rem(place + 1, tm_size), lax.rem(place + tm_size - 1, tm_size)
    over, under = lax.rem(place + 2, tm_size), lax.rem(place + tm_size - 2, tm_size)
    partner = 1 - column
    odd = lax.rem(place, 2) == 1
    even = lax.rem(place, 2) == 0
    has_left = place > 0
    has_right = place < tm_size - 1
    even_left = jnp.logical_and(even, has_left)
    even_right = jnp.logical_and(even, place < tm_size - 2)
    own_at = pl.ds(pl.multiple_of(column * half, half), half)
    other_at = pl.ds(pl.multiple_of(partner * half, half), half)
    rows = half // CHUNKS

    barrier = pltpu.get_barrier_semaphore()

    def greet(where):
        pl.semaphore_signal(barrier, inc=1, device_id=where, device_id_type=pl.DeviceIdType.MESH)

    greet((place, partner))
    pl.when(has_left)(lambda: greet((below, column)))
    pl.when(has_right)(lambda: greet((above, column)))
    pl.when(even_left)(lambda: greet((under, column)))
    pl.when(even_right)(lambda: greet((over, column)))
    peers = [x.astype(jnp.int32) for x in (has_left, has_right, even_left, even_right)]
    pl.semaphore_wait(barrier, 1 + peers[0] + peers[1] + peers[2] + peers[3])

    targets = {"above": (above, column), "below": (below, column), "partner": (place, partner), "over": (over, column)}

    def copy(slot, source, target, chunk=None):
        sem = CHUNKS * slot + (chunk or 0)
        if chunk is not None:
            at = slice(chunk * rows, (chunk + 1) * rows)
            source, landing = source.at[at], bufs.at[slot, at]
        else:
            landing = bufs.at[slot]
        return pltpu.make_async_remote_copy(
            src_ref=source, dst_ref=landing, send_sem=send_sem.at[sem], recv_sem=recv_sem.at[sem],
            device_id=targets[target], device_id_type=pl.DeviceIdType.MESH,
        )

    def assemble(into, own, other):
        into[own_at, :] = own[...]
        into[other_at, :] = other[...]

    def left(u, uother, f, d, s, dto, sto):
        z = split(z_ref[...])
        own, other = split(u[...]), split(uother[...])
        for values, base, out in ((own, d, dto), (split(f[...]), s, sto)):
            scaled = split(dot_parts(values, z, INNER))
            out[:, own_at] = base[:, own_at] - dot_parts(scaled, own, OUTER)
            out[:, other_at] = base[:, other_at] - dot_parts(scaled, other, OUTER)

    def right(u, f, dto, uto, sto):
        z = split(z_ref[...])
        onward = split(full_ref[...])
        turned = dot_parts(split(full_ref[:, own_at]), z, ((0,), (0,)))
        dto[...] = dto[...] - dot_parts(split(turned), onward, INNER)
        solved = dot_parts(split(f[...]), z, INNER)
        sto[...] = sto[...] - dot_parts(split(solved), onward, INNER)
        scaled = dot_parts(split(u[...]), z, INNER)
        uto[...] = -dot_parts(split(scaled), onward, INNER)

    c_do = copy(0, d_ref.at[1], "partner")
    c_uo = copy(1, u_ref.at[1], "partner")
    c_eo = copy(2, u_ref.at[0], "partner")
    c_ul = copy(3, u_ref.at[1], "above")
    c_fl = copy(4, f_ref.at[1], "above")
    c_zl = [copy(5, zown.at[0], "above", i) for i in range(CHUNKS)]
    c_zlo = [copy(6, bufs.at[5], "partner", i) for i in range(CHUNKS)]
    c_do.start()

    @pl.when(has_right)
    def _():
        c_ul.start()
        c_fl.start()

    c_uo.start()
    c_eo.start()
    c_do.wait_recv()
    assemble(s_ref, d_ref.at[1], bufs.at[0])
    invert(s_ref, tile_ref)
    zown[0] = s_ref[own_at, :]

    @pl.when(has_right)
    def _():
        for i in c_zl:
            i.start()

    c_uo.wait_recv()
    z_ref[...] = s_ref[...]
    left(u_ref.at[1], bufs.at[1], f_ref.at[1], d_ref.at[0], f_ref.at[0], cur.at[0], cur.at[2])
    c_eo.wait_recv()
    cur[1] = u_ref[0]

    @pl.when(has_left)
    def _():
        assemble(full_ref, u_ref.at[0], bufs.at[2])
        c_ul.wait_recv()
        c_fl.wait_recv()
        for i in range(CHUNKS):
            c_zl[i].wait_recv()
            c_zlo[i].start()
        for i in range(CHUNKS):
            c_zlo[i].wait_recv()
        assemble(z_ref, bufs.at[5], bufs.at[6])
        right(bufs.at[3], bufs.at[4], cur.at[0], cur.at[1], cur.at[2])

    c_do1 = copy(7, cur.at[0], "partner")
    c_uo1 = copy(8, cur.at[1], "partner")
    c_ua = copy(9, cur.at[1], "below")
    c_fa = copy(10, cur.at[2], "below")
    c_uao = copy(11, bufs.at[9], "partner")
    c_za = [copy(12, zown.at[1], "below", i) for i in range(CHUNKS)]
    c_zao = [copy(13, bufs.at[12], "partner", i) for i in range(CHUNKS)]
    c_ul1 = copy(14, bufs.at[9], "over")
    c_fl1 = copy(15, bufs.at[10], "over")
    c_zl1 = [copy(16, bufs.at[12], "over", i) for i in range(CHUNKS)]
    c_zl1o = [copy(17, bufs.at[16], "partner", i) for i in range(CHUNKS)]

    @pl.when(odd)
    def _():
        c_do1.start()
        c_ua.start()
        c_fa.start()
        c_do1.wait_recv()
        assemble(s_ref, cur.at[0], bufs.at[7])
        invert(s_ref, tile_ref)
        zown[1] = s_ref[own_at, :]
        for i in c_za:
            i.start()

        dout_ref[0] = cur[0]
        uout_ref[0] = cur[1]
        fout_ref[0] = cur[2]

    dout_ref[1] = d_ref[1]
    uout_ref[1] = u_ref[1]
    fout_ref[1] = f_ref[1]

    @pl.when(even)
    def _():
        c_uo1.start()
        c_ua.wait_recv()
        pl.when(even_right)(c_ul1.start)
        c_uao.start()
        c_uo1.wait_recv()
        assemble(full_ref, cur.at[1], bufs.at[8])
        uout_ref[0] = cur[1]
        c_fa.wait_recv()
        pl.when(even_right)(c_fl1.start)
        c_uao.wait_recv()
        for i in range(CHUNKS):
            c_za[i].wait_recv()
            pl.when(even_right)(c_zl1[i].start)
            c_zao[i].start()
        for i in range(CHUNKS):
            c_zao[i].wait_recv()
        assemble(z_ref, bufs.at[12], bufs.at[13])
        left(bufs.at[9], bufs.at[11], bufs.at[10], cur.at[0], cur.at[2], dout_ref.at[0], fout_ref.at[0])

    @pl.when(even_left)
    def _():
        c_ul1.wait_recv()
        c_fl1.wait_recv()
        for i in range(CHUNKS):
            c_zl1[i].wait_recv()
            c_zl1o[i].start()
        for i in range(CHUNKS):
            c_zl1o[i].wait_recv()
        assemble(z_ref, bufs.at[16], bufs.at[17])
        right(bufs.at[14], bufs.at[15], dout_ref.at[0], uout_ref.at[0], fout_ref.at[0])

    def drained(condition, copies):
        @pl.when(condition)
        def _():
            for i in copies:
                i.wait_send()

    for i in (c_do, c_uo, c_eo):
        i.wait_send()
    drained(has_right, [c_ul, c_fl] + c_zl)
    drained(has_left, c_zlo)
    drained(odd, [c_do1, c_ua, c_fa] + c_za)
    drained(even_right, [c_ul1, c_fl1] + c_zl1)
    drained(even, [c_uo1, c_uao] + c_zao)
    drained(even_left, c_zl1o)


SLOTS = 18


def body(tm_size, diagonal_blocks, upper_blocks, right_sides):
    shape = diagonal_blocks.shape
    half, size = shape[1], shape[2]
    whole = pl.BlockSpec(memory_space=pltpu.VMEM)
    return pl.pallas_call(
        functools.partial(kernel, tm_size),
        out_shape=[jax.ShapeDtypeStruct(shape, F32)] * 3,
        in_specs=[whole] * 3,
        out_specs=[whole] * 3,
        scratch_shapes=[
            pltpu.VMEM((size, size), F32),
            pltpu.VMEM((TILE, TILE), F32),
            pltpu.VMEM((size, size), F32),
            pltpu.VMEM((size, size), F32),
            pltpu.VMEM((2, half, size), F32),
            pltpu.VMEM((3, half, size), F32),
            pltpu.VMEM((SLOTS, half, size), F32),
            pltpu.SemaphoreType.DMA((SLOTS * CHUNKS,)),
            pltpu.SemaphoreType.DMA((SLOTS * CHUNKS,)),
        ],
        compiler_params=pltpu.CompilerParams(
            vmem_limit_bytes=50 * 2**20, collective_id=0, has_side_effects=True
        ),
        name="reduce_levels",
    )(diagonal_blocks, upper_blocks, right_sides)


def solution(mesh):
    placed = (P("tm", "col", None),) * 3
    return jax.shard_map(
        functools.partial(body, mesh.shape["tm"]),
        mesh=mesh,
        in_specs=placed,
        out_specs=placed,
        check_vma=False,
    )
```

profile of v0, /device:TPU:25, one launch (start us, length us, event | category | flops | bytes accessed | tf_op | source)
XLA Modules:
  0.0 102.6 jit_solution(17312872581870483226)
XLA Ops:
  0.6 99.0 %reduce_levels.1 = (f32[2,256,512]{2,1,0:T(8,128)S(1)}, f32[2,256,512]{2,1,0:T(8,128)S(1)}, f32[2,256,512]{2,1,0:T(8,128)S(1)}) custom-call(f32[2,256,512]{2,1,0:T(8,128)} %d_ref.1, f32[2,256,512]{2,1,0:T(8,128)} %u_ref.1, f32[2,256,512]{2,1,0:T(8,128)} %f_ref.1), custom_call_target="tpu_custom_call" | custom-call | tf_op jit(solution)/shard_map/reduce_levels/pallas_call | solution.py:323
  99.7 1.0 copy.9
  100.6 1.0 copy.10
  101.6 1.0 copy.11
where the time goes:
time: 103 us
  Pallas kernels  99 us (96%)
  local copies, waits for them, and re-layouts  2.91 us (3%)
    pallas_call x1, Pallas kernels, body(): pl.pallas_call(functools.partial(kernel, tm_size), out_shape=[jax.ShapeDt...  99 us
    unnamed x3, local copies, waits for them, and re-layouts  2.91 us

commit v1 on v0

--- a/solution.py
+++ b/solution.py
@@ -85,7 +85,6 @@
 
 INNER = ((1,), (0,))
 OUTER = ((1,), (1,))
-CHUNKS = 4
 
 
 def invert(s_ref, tile_ref):
@@ -120,7 +119,8 @@
 
 def kernel(
     tm_size, d_ref, u_ref, f_ref, dout_ref, uout_ref, fout_ref,
-    s_ref, tile_ref, z_ref, full_ref, zown, cur, bufs, send_sem, recv_sem,
+    s_ref, tile_ref, z_ref, full_ref, onward_ref, cur, scaled_ref, fresh_ref, ztiles, bufs, zbufs,
+    send_sem, recv_sem, zsend_sem, zrecv_sem,
 ):
     half, size = d_ref.shape[1], d_ref.shape[2]
     column = lax.axis_index("col")
@@ -132,11 +132,12 @@
     even = lax.rem(place, 2) == 0
     has_left = place > 0
     has_right = place < tm_size - 1
+    odd_right = jnp.logical_and(odd, has_right)
     even_left = jnp.logical_and(even, has_left)
     even_right = jnp.logical_and(even, place < tm_size - 2)
     own_at = pl.ds(pl.multiple_of(column * half, half), half)
     other_at = pl.ds(pl.multiple_of(partner * half, half), half)
-    rows = half // CHUNKS
+    tile = half // 2
 
     barrier = pltpu.get_barrier_semaphore()
 
@@ -153,29 +154,76 @@
 
     targets = {"above": (above, column), "below": (below, column), "partner": (place, partner), "over": (over, column)}
 
-    def copy(slot, source, target, chunk=None):
-        sem = CHUNKS * slot + (chunk or 0)
-        if chunk is not None:
-            at = slice(chunk * rows, (chunk + 1) * rows)
-            source, landing = source.at[at], bufs.at[slot, at]
-        else:
-            landing = bufs.at[slot]
+    def copy(slot, source, target, landing=None):
         return pltpu.make_async_remote_copy(
-            src_ref=source, dst_ref=landing, send_sem=send_sem.at[sem], recv_sem=recv_sem.at[sem],
+            src_ref=source, dst_ref=bufs.at[slot] if landing is None else landing,
+            send_sem=send_sem.at[slot], recv_sem=recv_sem.at[slot],
             device_id=targets[target], device_id_type=pl.DeviceIdType.MESH,
         )
+
+    def copy_tiles(slot, source, target):
+        return [
+            pltpu.make_async_remote_copy(
+                src_ref=source.at[i], dst_ref=zbufs.at[slot, i],
+                send_sem=zsend_sem.at[ZTILES * slot + i], recv_sem=zrecv_sem.at[ZTILES * slot + i],
+                device_id=targets[target], device_id_type=pl.DeviceIdType.MESH,
+            )
+            for i in range(ZTILES)
+        ]
 
     def assemble(into, own, other):
         into[own_at, :] = own[...]
         into[other_at, :] = other[...]
 
-    def left(u, uother, f, d, s, dto, sto):
+    def tile_places(c):
+        def at(row):
+            return pl.ds(pl.multiple_of(row, tile), tile)
+
+        first, far = c * half, (1 - c) * half
+        near = [at(first), at(first + tile)]
+        return [
+            (near[0], near[0]), (near[0], near[1]), (near[1], near[1]),
+            (near[0], at(far + c * tile)), (near[1], at(far + (1 - c) * tile)),
+        ]
+
+    def pack(z, into):
+        for i, (row, col) in enumerate(tile_places(column)):
+            into[i] = z[row, col]
+
+    def unpack(slot, c):
+        for i, (row, col) in enumerate(tile_places(c)):
+            value = zbufs[slot, i]
+            z_ref[row, col] = value
+            if i not in (0, 2):
+                z_ref[col, row] = value.T
+
+    def receive(slot, other_slot, arriving, shared, onward=None, condition=None):
+        for i in range(ZTILES):
+            arriving[i].wait_recv()
+            shared[i].start()
+            if onward is not None:
+                pl.when(condition)(onward[i].start)
+        unpack(slot, column)
+        for i in range(ZTILES):
+            shared[i].wait_recv()
+        unpack(other_slot, partner)
+
+    def left(u, uother, f, d, s, dto, sto, keep=None):
         z = split(z_ref[...])
         own, other = split(u[...]), split(uother[...])
-        for values, base, out in ((own, d, dto), (split(f[...]), s, sto)):
-            scaled = split(dot_parts(values, z, INNER))
+        for n, (values, base, out) in enumerate(((own, d, dto), (split(f[...]), s, sto))):
+            scaled = dot_parts(values, z, INNER)
+            if keep is not None:
+                keep[n] = scaled
+            scaled = split(scaled)
             out[:, own_at] = base[:, own_at] - dot_parts(scaled, own, OUTER)
             out[:, other_at] = base[:, other_at] - dot_parts(scaled, other, OUTER)
+
+    def right_block(dto):
+        z = split(z_ref[...])
+        onward = split(full_ref[...])
+        turned = dot_parts(split(full_ref[:, own_at]), z, ((0,), (0,)))
+        dto[...] = dto[...] - dot_parts(split(turned), onward, INNER)
 
     def right(u, f, dto, uto, sto):
         z = split(z_ref[...])
@@ -187,16 +235,32 @@
         scaled = dot_parts(split(u[...]), z, INNER)
         uto[...] = -dot_parts(split(scaled), onward, INNER)
 
-    c_do = copy(0, d_ref.at[1], "partner")
-    c_uo = copy(1, u_ref.at[1], "partner")
-    c_eo = copy(2, u_ref.at[0], "partner")
-    c_ul = copy(3, u_ref.at[1], "above")
-    c_fl = copy(4, f_ref.at[1], "above")
-    c_zl = [copy(5, zown.at[0], "above", i) for i in range(CHUNKS)]
-    c_zlo = [copy(6, bufs.at[5], "partner", i) for i in range(CHUNKS)]
+    c_do = copy(DO, d_ref.at[1], "partner")
+    c_uo = copy(UO, u_ref.at[1], "partner")
+    c_eo = copy(EO, u_ref.at[0], "partner")
+    c_e = copy(EB, u_ref.at[0], "below")
+    c_ex = copy(EX, bufs.at[EB], "partner")
+    c_ul = copy(UL, u_ref.at[1], "above")
+    c_fl = copy(FL, f_ref.at[1], "above")
+    c_fb = copy(FB, cur.at[2], "below")
+    c_do1 = copy(DO1, cur.at[0], "partner")
+    c_uo1 = copy(UO1, cur.at[1], "partner")
+    c_uao = copy(UAO, fresh_ref.at[0], "partner")
+    c_ul1 = copy(UL1, fresh_ref.at[0], "over")
+    c_fl1 = copy(FL1, fresh_ref.at[1], "over")
+    c_ru = copy(RU, fresh_ref.at[0], "above", uout_ref.at[0])
+    c_rf = copy(RF, fresh_ref.at[1], "above", fout_ref.at[0])
+    c_zl = copy_tiles(ZL, ztiles.at[0], "above")
+    c_zlo = copy_tiles(ZLO, zbufs.at[ZL], "partner")
+    c_za = copy_tiles(ZA, ztiles.at[1], "below")
+    c_zao = copy_tiles(ZAO, zbufs.at[ZA], "partner")
+    c_zl1 = copy_tiles(ZL1, zbufs.at[ZA], "over")
+    c_zl1o = copy_tiles(ZL1O, zbufs.at[ZL1], "partner")
+
     c_do.start()
-
-    @pl.when(has_right)
+    pl.when(odd)(c_e.start)
+
+    @pl.when(odd_right)
     def _():
         c_ul.start()
         c_fl.start()
@@ -204,9 +268,9 @@
     c_uo.start()
     c_eo.start()
     c_do.wait_recv()
-    assemble(s_ref, d_ref.at[1], bufs.at[0])
+    assemble(s_ref, d_ref.at[1], bufs.at[DO])
     invert(s_ref, tile_ref)
-    zown[0] = s_ref[own_at, :]
+    pack(s_ref, ztiles.at[0])
 
     @pl.when(has_right)
     def _():
@@ -215,87 +279,70 @@
 
     c_uo.wait_recv()
     z_ref[...] = s_ref[...]
-    left(u_ref.at[1], bufs.at[1], f_ref.at[1], d_ref.at[0], f_ref.at[0], cur.at[0], cur.at[2])
+    left(
+        u_ref.at[1], bufs.at[UO], f_ref.at[1], d_ref.at[0], f_ref.at[0], cur.at[0], cur.at[2], scaled_ref
+    )
     c_eo.wait_recv()
-    cur[1] = u_ref[0]
-
-    @pl.when(has_left)
-    def _():
-        assemble(full_ref, u_ref.at[0], bufs.at[2])
-        c_ul.wait_recv()
-        c_fl.wait_recv()
-        for i in range(CHUNKS):
-            c_zl[i].wait_recv()
-            c_zlo[i].start()
-        for i in range(CHUNKS):
-            c_zlo[i].wait_recv()
-        assemble(z_ref, bufs.at[5], bufs.at[6])
-        right(bufs.at[3], bufs.at[4], cur.at[0], cur.at[1], cur.at[2])
-
-    c_do1 = copy(7, cur.at[0], "partner")
-    c_uo1 = copy(8, cur.at[1], "partner")
-    c_ua = copy(9, cur.at[1], "below")
-    c_fa = copy(10, cur.at[2], "below")
-    c_uao = copy(11, bufs.at[9], "partner")
-    c_za = [copy(12, zown.at[1], "below", i) for i in range(CHUNKS)]
-    c_zao = [copy(13, bufs.at[12], "partner", i) for i in range(CHUNKS)]
-    c_ul1 = copy(14, bufs.at[9], "over")
-    c_fl1 = copy(15, bufs.at[10], "over")
-    c_zl1 = [copy(16, bufs.at[12], "over", i) for i in range(CHUNKS)]
-    c_zl1o = [copy(17, bufs.at[16], "partner", i) for i in range(CHUNKS)]
-
-    @pl.when(odd)
-    def _():
-        c_do1.start()
-        c_ua.start()
-        c_fa.start()
-        c_do1.wait_recv()
-        assemble(s_ref, cur.at[0], bufs.at[7])
-        invert(s_ref, tile_ref)
-        zown[1] = s_ref[own_at, :]
-        for i in c_za:
-            i.start()
-
-        dout_ref[0] = cur[0]
-        uout_ref[0] = cur[1]
-        fout_ref[0] = cur[2]
-
+    assemble(full_ref, u_ref.at[0], bufs.at[EO])
     dout_ref[1] = d_ref[1]
     uout_ref[1] = u_ref[1]
     fout_ref[1] = f_ref[1]
 
+    @pl.when(odd)
+    def _():
+        c_fb.start()
+        receive(ZL, ZLO, c_zl, c_zlo)
+        right_block(cur.at[0])
+        c_do1.start()
+        dout_ref[0] = cur[0]
+        c_do1.wait_recv()
+        assemble(s_ref, cur.at[0], bufs.at[DO1])
+        invert(s_ref, tile_ref)
+        pack(s_ref, ztiles.at[1])
+        for i in c_za:
+            i.start()
+        c_ru.wait_recv()
+        c_rf.wait_recv()
+
     @pl.when(even)
     def _():
+        c_e.wait_recv()
+        c_ex.start()
+        c_ex.wait_recv()
+        assemble(onward_ref, bufs.at[EB], bufs.at[EX])
+        fresh_ref[0] = -dot3(scaled_ref[0], onward_ref[...])
+        c_ru.start()
+        c_uao.start()
+        pl.when(even_right)(c_ul1.start)
+        cur[1] = u_ref[0]
+
+        @pl.when(has_left)
+        def _():
+            c_ul.wait_recv()
+            c_fl.wait_recv()
+            receive(ZL, ZLO, c_zl, c_zlo)
+            right(bufs.at[UL], bufs.at[FL], cur.at[0], cur.at[1], cur.at[2])
+
         c_uo1.start()
-        c_ua.wait_recv()
-        pl.when(even_right)(c_ul1.start)
-        c_uao.start()
+        c_fb.wait_recv()
+        fresh_ref[1] = bufs[FB] - dot3(scaled_ref[1], onward_ref[...])
+        c_rf.start()
+        pl.when(even_right)(c_fl1.start)
         c_uo1.wait_recv()
-        assemble(full_ref, cur.at[1], bufs.at[8])
+        assemble(full_ref, cur.at[1], bufs.at[UO1])
         uout_ref[0] = cur[1]
-        c_fa.wait_recv()
-        pl.when(even_right)(c_fl1.start)
         c_uao.wait_recv()
-        for i in range(CHUNKS):
-            c_za[i].wait_recv()
-            pl.when(even_right)(c_zl1[i].start)
-            c_zao[i].start()
-        for i in range(CHUNKS):
-            c_zao[i].wait_recv()
-        assemble(z_ref, bufs.at[12], bufs.at[13])
-        left(bufs.at[9], bufs.at[11], bufs.at[10], cur.at[0], cur.at[2], dout_ref.at[0], fout_ref.at[0])
+        receive(ZA, ZAO, c_za, c_zao, c_zl1, even_right)
+        left(
+            fresh_ref.at[0], bufs.at[UAO], fresh_ref.at[1], cur.at[0], cur.at[2], dout_ref.at[0], fout_ref.at[0]
+        )
 
     @pl.when(even_left)
     def _():
         c_ul1.wait_recv()
         c_fl1.wait_recv()
-        for i in range(CHUNKS):
-            c_zl1[i].wait_recv()
-            c_zl1o[i].start()
-        for i in range(CHUNKS):
-            c_zl1o[i].wait_recv()
-        assemble(z_ref, bufs.at[16], bufs.at[17])
-        right(bufs.at[14], bufs.at[15], dout_ref.at[0], uout_ref.at[0], fout_ref.at[0])
+        receive(ZL1, ZL1O, c_zl1, c_zl1o)
+        right(bufs.at[UL1], bufs.at[FL1], dout_ref.at[0], uout_ref.at[0], fout_ref.at[0])
 
     def drained(condition, copies):
         @pl.when(condition)
@@ -305,20 +352,26 @@
 
     for i in (c_do, c_uo, c_eo):
         i.wait_send()
-    drained(has_right, [c_ul, c_fl] + c_zl)
+    drained(has_right, c_zl)
     drained(has_left, c_zlo)
-    drained(odd, [c_do1, c_ua, c_fa] + c_za)
+    drained(odd_right, [c_ul, c_fl])
+    drained(odd, [c_e, c_fb, c_do1] + c_za)
+    drained(even, [c_ex, c_ru, c_rf, c_uao, c_uo1] + c_zao)
     drained(even_right, [c_ul1, c_fl1] + c_zl1)
-    drained(even, [c_uo1, c_uao] + c_zao)
     drained(even_left, c_zl1o)
 
 
-SLOTS = 18
+SLOTS = 15
+DO, UO, EO, EB, EX, UL, FL, FB, DO1, UO1, UAO, UL1, FL1, RU, RF = range(SLOTS)
+ZSLOTS = 6
+ZL, ZLO, ZA, ZAO, ZL1, ZL1O = range(ZSLOTS)
+ZTILES = 5
 
 
 def body(tm_size, diagonal_blocks, upper_blocks, right_sides):
     shape = diagonal_blocks.shape
     half, size = shape[1], shape[2]
+    tile = half // 2
     whole = pl.BlockSpec(memory_space=pltpu.VMEM)
     return pl.pallas_call(
         functools.partial(kernel, tm_size),
@@ -330,11 +383,17 @@
             pltpu.VMEM((TILE, TILE), F32),
             pltpu.VMEM((size, size), F32),
             pltpu.VMEM((size, size), F32),
+            pltpu.VMEM((size, size), F32),
+            pltpu.VMEM((3, half, size), F32),
             pltpu.VMEM((2, half, size), F32),
-            pltpu.VMEM((3, half, size), F32),
-            pltpu.VMEM((SLOTS, half, size), F32),
-            pltpu.SemaphoreType.DMA((SLOTS * CHUNKS,)),
-            pltpu.SemaphoreType.DMA((SLOTS * CHUNKS,)),
+            pltpu.VMEM((2, half, size), F32),
+            pltpu.VMEM((2, ZTILES, tile, tile), F32),
+            pltpu.VMEM((RU, half, size), F32),
+            pltpu.VMEM((ZSLOTS, ZTILES, tile, tile), F32),
+            pltpu.SemaphoreType.DMA((SLOTS,)),
+            pltpu.SemaphoreType.DMA((SLOTS,)),
+            pltpu.SemaphoreType.DMA((ZSLOTS * ZTILES,)),
+            pltpu.SemaphoreType.DMA((ZSLOTS * ZTILES,)),
         ],
         compiler_params=pltpu.CompilerParams(
             vmem_limit_bytes=50 * 2**20, collective_id=0, has_side_effects=True

time: 103 us -> 89.4 us (0.87)
  Pallas kernels: 99 us -> 85.7 us
    pallas_call x1, Pallas kernels: 99 us -> 85.7 us  [body(): pl.pallas_call(functools.partial(kernel, tm_size), out_shape=[jax.ShapeDt...]
where the time goes in v1:
time: 89.4 us; the launch traced here: 89.2 us
  Pallas kernels  85.7 us (96%)
  local copies, waits for them, and re-layouts  2.91 us (3%)
    pallas_call x1, Pallas kernels, body(): pl.pallas_call(functools.partial(kernel, tm_size), out_shape=[jax.ShapeDt...  85.7 us
    unnamed x3, local copies, waits for them, and re-layouts  2.91 us

profile of v1, /device:TPU:25, one launch (start us, length us, event | category | flops | bytes accessed | tf_op | source)
XLA Modules:
  0.0 89.2 jit_solution(3307458160515006870)
XLA Ops:
  0.6 85.7 %reduce_levels.1 = (f32[2,256,512]{2,1,0:T(8,128)S(1)}, f32[2,256,512]{2,1,0:T(8,128)S(1)}, f32[2,256,512]{2,1,0:T(8,128)S(1)}) custom-call(f32[2,256,512]{2,1,0:T(8,128)} %d_ref.1, f32[2,256,512]{2,1,0:T(8,128)} %u_ref.1, f32[2,256,512]{2,1,0:T(8,128)} %f_ref.1), custom_call_target="tpu_custom_call" | custom-call | tf_op jit(solution)/shard_map/reduce_levels/pallas_call | solution.py:376
  86.3 1.0 %copy.9 = f32[2,256,512]{2,1,0:T(8,128)} copy(f32[2,256,512]{2,1,0:T(8,128)S(1)} %get-tuple-element.6) | data formatting | bytes 2097152
  87.3 1.0 %copy.10 = f32[2,256,512]{2,1,0:T(8,128)} copy(f32[2,256,512]{2,1,0:T(8,128)S(1)} %get-tuple-element.7) | data formatting | bytes 2097152
  88.2 1.0 %copy.11 = f32[2,256,512]{2,1,0:T(8,128)} copy(f32[2,256,512]{2,1,0:T(8,128)S(1)} %get-tuple-element.8) | data formatting | bytes 2097152

commit v2 on v1

--- a/solution.py
+++ b/solution.py
@@ -87,40 +87,74 @@
 OUTER = ((1,), (1,))
 
 
-def invert(s_ref, tile_ref):
-    size = s_ref.shape[0]
-    blocks = size // TILE
-
-    @pl.loop(0, blocks)
+def invert(s_ref, tile_ref, fac_ref, col_ref, ready, send):
+    blocks = s_ref.shape[0] // TILE
+    steps = TILE // PANEL
+
+    def span(index):
+        return pl.ds(pl.multiple_of(index * TILE, TILE), TILE)
+
+    def fixed(index):
+        return slice(index * TILE, (index + 1) * TILE)
+
+    def take_column(k):
+        for o in range(blocks - 1):
+            rat = span(lax.rem(k + o + 1, blocks))
+            col_ref[o] = s_ref[rat, span(k)]
+            s_ref[rat, span(k)] = jnp.zeros((TILE, TILE), F32)
+
+    def row_job(k, c):
+        inverse = tile_ref[...]
+        value = jnp.where(k == c, inverse, dot3(inverse, s_ref[span(k), fixed(c)]))
+        fac_ref[k, c] = value
+        s_ref[span(k), fixed(c)] = value
+
+    def update_job(k, o, c):
+        rat = span(lax.rem(k + o + 1, blocks))
+        s_ref[rat, fixed(c)] = s_ref[rat, fixed(c)] - dot3(col_ref[o], fac_ref[k, c])
+
+    def invert_tile(k, jobs):
+        groups = [
+            s_ref[pl.ds(pl.multiple_of(k * TILE, TILE) + PANEL * g, PANEL), span(k)] for g in range(steps)
+        ]
+        for p in range(steps):
+            groups = panel_step(groups, p)
+            for job in jobs[p * len(jobs) // steps : (p + 1) * len(jobs) // steps]:
+                job()
+        for g in range(steps):
+            tile_ref[PANEL * g : PANEL * (g + 1), :] = groups[g]
+
+    invert_tile(0, [])
+    ready()
+
+    @pl.loop(1, blocks)
     def _(k):
-        at = pl.ds(pl.multiple_of(k * TILE, TILE), TILE)
-        groups = [
-            s_ref[pl.ds(pl.multiple_of(k * TILE, TILE) + PANEL * g, PANEL), at]
-            for g in range(TILE // PANEL)
-        ]
-        for p in range(TILE // PANEL):
-            groups = panel_step(groups, p)
-        for g in range(TILE // PANEL):
-            tile_ref[PANEL * g : PANEL * (g + 1), :] = groups[g]
-        inverse = tile_ref[...]
-        row = dot3(inverse, s_ref[at, :])
-        s_ref[at, :] = row
-        s_ref[at, at] = inverse
-        row_parts = split(s_ref[at, :])
-        for r in range(blocks):
-
-            @pl.when(r != k)
-            def _():
-                rat = slice(r * TILE, (r + 1) * TILE)
-                column = s_ref[rat, at]
-                s_ref[rat, at] = jnp.zeros((TILE, TILE), F32)
-                s_ref[rat, :] = s_ref[rat, :] - dot_parts(split(column), row_parts, INNER)
+        last = k - 1
+        take_column(last)
+        row = dot3(tile_ref[...], s_ref[span(last), span(k)])
+        s_ref[span(k), span(k)] = s_ref[span(k), span(k)] - dot3(col_ref[0], row)
+        jobs = [functools.partial(row_job, last, c) for c in range(blocks)]
+        jobs.append(lambda: send(last))
+        for o in range(blocks - 1):
+            jobs += [functools.partial(update_job, last, o, c) for c in range(blocks)]
+        invert_tile(k, jobs)
+
+    end = blocks - 1
+    fac_ref[end, end] = tile_ref[...]
+    send(end)
+    take_column(end)
+    s_ref[fixed(end), fixed(end)] = tile_ref[...]
+    for c in range(end):
+        row_job(end, c)
+    for o in range(blocks - 1):
+        for c in range(blocks):
+            update_job(end, o, c)
 
 
 def kernel(
     tm_size, d_ref, u_ref, f_ref, dout_ref, uout_ref, fout_ref,
-    s_ref, tile_ref, z_ref, full_ref, onward_ref, cur, scaled_ref, fresh_ref, ztiles, bufs, zbufs,
-    send_sem, recv_sem, zsend_sem, zrecv_sem,
+    s_ref, tile_ref, fac_ref, col_ref, z_ref, full_ref, onward_ref, cur, scaled_ref, fresh_ref, ztiles, bufs, zbufs, fbufs,
+    send_sem, recv_sem, zsend_sem, zrecv_sem, fsend_sem, frecv_sem,
 ):
     half, size = d_ref.shape[1], d_ref.shape[2]
     column = lax.axis_index("col")
@@ -186,9 +220,38 @@
             (near[0], at(far + c * tile)), (near[1], at(far + (1 - c) * tile)),
         ]
 
-    def pack(z, into):
-        for i, (row, col) in enumerate(tile_places(column)):
-            into[i] = z[row, col]
+    def pack(into):
+        places = [(0, 0), (0, tile), (tile, tile), (0, half + column * tile), (tile, half + partner * tile)]
+        for i, (row, col) in enumerate(places):
+            into[i] = s_ref[row : row + tile, pl.ds(pl.multiple_of(col, tile), tile)]
+
+    def fill_own(source):
+        s_ref[:half, :half] = source[:, own_at]
+        s_ref[:half, half:] = source[:, other_at]
+
+    def fill_other(source):
+        s_ref[half:, :half] = source[:, own_at]
+        s_ref[half:, half:] = source[:, other_at]
+
+    def store_inverse():
+        z_ref[own_at, own_at] = s_ref[:half, :half]
+        z_ref[own_at, other_at] = s_ref[:half, half:]
+        z_ref[other_at, own_at] = s_ref[half:, :half]
+        z_ref[other_at, other_at] = s_ref[half:, half:]
+
+    blocks = size // TILE
+
+    def copy_factor(k, c):
+        sem = k * blocks + c
+        return pltpu.make_async_remote_copy(
+            src_ref=fac_ref.at[k, c], dst_ref=fbufs.at[k, c],
+            send_sem=fsend_sem.at[sem], recv_sem=frecv_sem.at[sem],
+            device_id=targets["above"], device_id_type=pl.DeviceIdType.MESH,
+        )
+
+    def send_factor(k):
+        for c in range(blocks):
+            pl.when(jnp.logical_and(even, c >= k))(copy_factor(k, c).start)
 
     def unpack(slot, c):
         for i, (row, col) in enumerate(tile_places(c)):
@@ -220,10 +283,15 @@
             out[:, other_at] = base[:, other_at] - dot_parts(scaled, other, OUTER)
 
     def right_block(dto):
-        z = split(z_ref[...])
-        onward = split(full_ref[...])
-        turned = dot_parts(split(full_ref[:, own_at]), z, ((0,), (0,)))
-        dto[...] = dto[...] - dot_parts(split(turned), onward, INNER)
+        for m in range(blocks):
+            at = slice(m * TILE, (m + 1) * TILE)
+            for c in range(m, blocks):
+                copy_factor(m, c).wait_recv()
+            onward_ref[at] = dot3(fbufs[m, m], full_ref[at])
+            for c in range(m + 1, blocks):
+                rat = slice(c * TILE, (c + 1) * TILE)
+                full_ref[rat] = full_ref[rat] - dot3(fbufs[m, c], full_ref[at], ((0,), (0,)))
+        dto[...] = dto[...] - dot3(full_ref[:, own_at], onward_ref[...], ((0,), (0,)))
 
     def right(u, f, dto, uto, sto):
         z = split(z_ref[...])
@@ -267,23 +335,26 @@
 
     c_uo.start()
     c_eo.start()
-    c_do.wait_recv()
-    assemble(s_ref, d_ref.at[1], bufs.at[DO])
-    invert(s_ref, tile_ref)
-    pack(s_ref, ztiles.at[0])
-
-    @pl.when(has_right)
+    fill_own(d_ref.at[1])
+
+    def ready():
+        c_do.wait_recv()
+        fill_other(bufs.at[DO])
+
+    invert(s_ref, tile_ref, fac_ref, col_ref, ready, send_factor)
+
+    @pl.when(odd_right)
     def _():
+        pack(ztiles.at[0])
         for i in c_zl:
             i.start()
 
+    store_inverse()
     c_uo.wait_recv()
-    z_ref[...] = s_ref[...]
     left(
         u_ref.at[1], bufs.at[UO], f_ref.at[1], d_ref.at[0], f_ref.at[0], cur.at[0], cur.at[2], scaled_ref
     )
     c_eo.wait_recv()
-    assemble(full_ref, u_ref.at[0], bufs.at[EO])
     dout_ref[1] = d_ref[1]
     uout_ref[1] = u_ref[1]
     fout_ref[1] = f_ref[1]
@@ -291,14 +362,19 @@
     @pl.when(odd)
     def _():
         c_fb.start()
-        receive(ZL, ZLO, c_zl, c_zlo)
+        full_ref[:half] = u_ref[0]
+        full_ref[half:] = bufs[EO]
         right_block(cur.at[0])
         c_do1.start()
-        dout_ref[0] = cur[0]
-        c_do1.wait_recv()
-        assemble(s_ref, cur.at[0], bufs.at[DO1])
-        invert(s_ref, tile_ref)
-        pack(s_ref, ztiles.at[1])
+        fill_own(cur.at[0])
+
+        def ready():
+            c_do1.wait_recv()
+            fill_other(bufs.at[DO1])
+            dout_ref[0] = cur[0]
+
+        invert(s_ref, tile_ref, fac_ref, col_ref, ready, lambda k: None)
+        pack(ztiles.at[1])
         for i in c_za:
             i.start()
         c_ru.wait_recv()
@@ -321,6 +397,7 @@
             c_ul.wait_recv()
             c_fl.wait_recv()
             receive(ZL, ZLO, c_zl, c_zlo)
+            assemble(full_ref, u_ref.at[0], bufs.at[EO])
             right(bufs.at[UL], bufs.at[FL], cur.at[0], cur.at[1], cur.at[2])
 
         c_uo1.start()
@@ -352,9 +429,9 @@
 
     for i in (c_do, c_uo, c_eo):
         i.wait_send()
-    drained(has_right, c_zl)
-    drained(has_left, c_zlo)
-    drained(odd_right, [c_ul, c_fl])
+    drained(odd_right, [c_ul, c_fl] + c_zl)
+    drained(even_left, c_zlo)
+    drained(even, [copy_factor(k, c) for k in range(blocks) for c in range(k, blocks)])
     drained(odd, [c_e, c_fb, c_do1] + c_za)
     drained(even, [c_ex, c_ru, c_rf, c_uao, c_uo1] + c_zao)
     drained(even_right, [c_ul1, c_fl1] + c_zl1)
@@ -371,7 +448,7 @@
 def body(tm_size, diagonal_blocks, upper_blocks, right_sides):
     shape = diagonal_blocks.shape
     half, size = shape[1], shape[2]
-    tile = half // 2
+    tile, blocks = half // 2, size // TILE
     whole = pl.BlockSpec(memory_space=pltpu.VMEM)
     return pl.pallas_call(
         functools.partial(kernel, tm_size),
@@ -381,6 +458,8 @@
         scratch_shapes=[
             pltpu.VMEM((size, size), F32),
             pltpu.VMEM((TILE, TILE), F32),
+            pltpu.VMEM((blocks, blocks, TILE, TILE), F32),
+            pltpu.VMEM((blocks - 1, TILE, TILE), F32),
             pltpu.VMEM((size, size), F32),
             pltpu.VMEM((size, size), F32),
             pltpu.VMEM((size, size), F32),
@@ -390,10 +469,13 @@
             pltpu.VMEM((2, ZTILES, tile, tile), F32),
             pltpu.VMEM((RU, half, size), F32),
             pltpu.VMEM((ZSLOTS, ZTILES, tile, tile), F32),
+            pltpu.VMEM((blocks, blocks, TILE, TILE), F32),
             pltpu.SemaphoreType.DMA((SLOTS,)),
             pltpu.SemaphoreType.DMA((SLOTS,)),
             pltpu.SemaphoreType.DMA((ZSLOTS * ZTILES,)),
             pltpu.SemaphoreType.DMA((ZSLOTS * ZTILES,)),
+            pltpu.SemaphoreType.DMA((blocks * blocks,)),
+            pltpu.SemaphoreType.DMA((blocks * blocks,)),
         ],
         compiler_params=pltpu.CompilerParams(
             vmem_limit_bytes=50 * 2**20, collective_id=0, has_side_effects=True

time: 89.4 us -> 89.7 us (level)
  no operation moved by 1% of the time
where the time goes in v2:
time: 89.7 us; the launch traced here: 89.5 us
  Pallas kernels  86 us (96%)
  local copies, waits for them, and re-layouts  2.91 us (3%)
    pallas_call x1, Pallas kernels, body(): pl.pallas_call(functools.partial(kernel, tm_size), out_shape=[jax.ShapeDt...  86 us
    unnamed x3, local copies, waits for them, and re-layouts  2.91 us

profile of v2, /device:TPU:25, one launch (start us, length us, event | category | flops | bytes accessed | tf_op | source)
XLA Modules:
  0.0 89.5 jit_solution(16900128057972761691)
XLA Ops:
  0.6 86.0 %reduce_levels.1 = (f32[2,256,512]{2,1,0:T(8,128)S(1)}, f32[2,256,512]{2,1,0:T(8,128)S(1)}, f32[2,256,512]{2,1,0:T(8,128)S(1)}) custom-call(f32[2,256,512]{2,1,0:T(8,128)} %d_ref.1, f32[2,256,512]{2,1,0:T(8,128)} %u_ref.1, f32[2,256,512]{2,1,0:T(8,128)} %f_ref.1), custom_call_target="tpu_custom_call" | custom-call | tf_op jit(solution)/shard_map/reduce_levels/pallas_call | solution.py:453
  86.6 1.0 %copy.9 = f32[2,256,512]{2,1,0:T(8,128)} copy(f32[2,256,512]{2,1,0:T(8,128)S(1)} %get-tuple-element.6) | data formatting | bytes 2097152
  87.6 1.0 %copy.10 = f32[2,256,512]{2,1,0:T(8,128)} copy(f32[2,256,512]{2,1,0:T(8,128)S(1)} %get-tuple-element.7) | data formatting | bytes 2097152
  88.5 1.0 %copy.11 = f32[2,256,512]{2,1,0:T(8,128)} copy(f32[2,256,512]{2,1,0:T(8,128)S(1)} %get-tuple-element.8) | data formatting | bytes 2097152

commit v3 on v2

--- a/solution.py
+++ b/solution.py
@@ -87,7 +87,7 @@
 OUTER = ((1,), (1,))
 
 
-def invert(s_ref, tile_ref, fac_ref, col_ref, ready, send):
+def invert(s_ref, tile_ref, fac_ref, col_ref, ready, send, after):
     blocks = s_ref.shape[0] // TILE
     steps = TILE // PANEL
 
@@ -138,6 +138,7 @@
         for o in range(blocks - 1):
             jobs += [functools.partial(update_job, last, o, c) for c in range(blocks)]
         invert_tile(k, jobs)
+        after(k)
 
     end = blocks - 1
     fac_ref[end, end] = tile_ref[...]
@@ -153,7 +154,7 @@
 
 def kernel(
     tm_size, d_ref, u_ref, f_ref, dout_ref, uout_ref, fout_ref,
-    s_ref, tile_ref, fac_ref, col_ref, z_ref, full_ref, onward_ref, cur, scaled_ref, fresh_ref, ztiles, bufs, zbufs, fbufs,
+    s_ref, tile_ref, fac_ref, col_ref, z_ref, full_ref, onward_ref, ahead_ref, cur, scaled_ref, fresh_ref, ztiles, bufs, zbufs, fbufs,
     send_sem, recv_sem, zsend_sem, zrecv_sem, fsend_sem, frecv_sem,
 ):
     half, size = d_ref.shape[1], d_ref.shape[2]
@@ -166,9 +167,11 @@
     even = lax.rem(place, 2) == 0
     has_left = place > 0
     has_right = place < tm_size - 1
-    odd_right = jnp.logical_and(odd, has_right)
-    even_left = jnp.logical_and(even, has_left)
-    even_right = jnp.logical_and(even, place < tm_size - 2)
+    has_under, has_over = place > 1, place < tm_size - 2
+    odd_over = jnp.logical_and(odd, has_over)
+    odd_under = jnp.logical_and(odd, has_under)
+    even_left = jnp.logical_and(even, has_under)
+    even_right = jnp.logical_and(even, has_over)
     own_at = pl.ds(pl.multiple_of(column * half, half), half)
     other_at = pl.ds(pl.multiple_of(partner * half, half), half)
     tile = half // 2
@@ -181,9 +184,9 @@
     greet((place, partner))
     pl.when(has_left)(lambda: greet((below, column)))
     pl.when(has_right)(lambda: greet((above, column)))
-    pl.when(even_left)(lambda: greet((under, column)))
-    pl.when(even_right)(lambda: greet((over, column)))
-    peers = [x.astype(jnp.int32) for x in (has_left, has_right, even_left, even_right)]
+    pl.when(has_under)(lambda: greet((under, column)))
+    pl.when(has_over)(lambda: greet((over, column)))
+    peers = [x.astype(jnp.int32) for x in (has_left, has_right, has_under, has_over)]
     pl.semaphore_wait(barrier, 1 + peers[0] + peers[1] + peers[2] + peers[3])
 
     targets = {"above": (above, column), "below": (below, column), "partner": (place, partner), "over": (over, column)}
@@ -293,23 +296,30 @@
                 full_ref[rat] = full_ref[rat] - dot3(fbufs[m, c], full_ref[at], ((0,), (0,)))
         dto[...] = dto[...] - dot3(full_ref[:, own_at], onward_ref[...], ((0,), (0,)))
 
-    def right(u, f, dto, uto, sto):
-        z = split(z_ref[...])
-        onward = split(full_ref[...])
-        turned = dot_parts(split(full_ref[:, own_at]), z, ((0,), (0,)))
-        dto[...] = dto[...] - dot_parts(split(turned), onward, INNER)
-        solved = dot_parts(split(f[...]), z, INNER)
-        sto[...] = sto[...] - dot_parts(split(solved), onward, INNER)
-        scaled = dot_parts(split(u[...]), z, INNER)
-        uto[...] = -dot_parts(split(scaled), onward, INNER)
+    def ahead(into):
+        into[...] = dot3(z_ref[...], full_ref[...])
+
+    def right(product_ref, u, dto, uto):
+        product = split(product_ref[...])
+        dto[...] = dto[...] - dot_parts(split(full_ref[:, own_at]), product, ((0,), (0,)))
+        uto[...] = -dot_parts(split(u[...]), product, INNER)
+
+    def right_source(product_ref, f, sto):
+        sto[...] = sto[...] - dot3(f[...], product_ref[...])
 
     c_do = copy(DO, d_ref.at[1], "partner")
     c_uo = copy(UO, u_ref.at[1], "partner")
     c_eo = copy(EO, u_ref.at[0], "partner")
     c_e = copy(EB, u_ref.at[0], "below")
     c_ex = copy(EX, bufs.at[EB], "partner")
-    c_ul = copy(UL, u_ref.at[1], "above")
-    c_fl = copy(FL, f_ref.at[1], "above")
+    c_ulr = copy(ULR, u_ref.at[1], "over")
+    c_flr = copy(FLR, f_ref.at[1], "over")
+    c_ulf = copy(UL, bufs.at[ULR], "below")
+    top, low = slice(0, half // 2), slice(half // 2, half)
+    c_flf = [
+        copy(FL, bufs.at[FLR, top], "below", bufs.at[FL, top]),
+        copy(FL2, bufs.at[FLR, low], "below", bufs.at[FL, low]),
+    ]
     c_fb = copy(FB, cur.at[2], "below")
     c_do1 = copy(DO1, cur.at[0], "partner")
     c_uo1 = copy(UO1, cur.at[1], "partner")
@@ -318,7 +328,8 @@
     c_fl1 = copy(FL1, fresh_ref.at[1], "over")
     c_ru = copy(RU, fresh_ref.at[0], "above", uout_ref.at[0])
     c_rf = copy(RF, fresh_ref.at[1], "above", fout_ref.at[0])
-    c_zl = copy_tiles(ZL, ztiles.at[0], "above")
+    c_zlr = copy_tiles(ZLR, ztiles.at[0], "over")
+    c_zl = copy_tiles(ZL, zbufs.at[ZLR], "below")
     c_zlo = copy_tiles(ZLO, zbufs.at[ZL], "partner")
     c_za = copy_tiles(ZA, ztiles.at[1], "below")
     c_zao = copy_tiles(ZAO, zbufs.at[ZA], "partner")
@@ -328,11 +339,7 @@
     c_do.start()
     pl.when(odd)(c_e.start)
 
-    @pl.when(odd_right)
-    def _():
-        c_ul.start()
-        c_fl.start()
-
+    pl.when(odd_over)(c_ulr.start)
     c_uo.start()
     c_eo.start()
     fill_own(d_ref.at[1])
@@ -341,12 +348,20 @@
         c_do.wait_recv()
         fill_other(bufs.at[DO])
 
-    invert(s_ref, tile_ref, fac_ref, col_ref, ready, send_factor)
-
-    @pl.when(odd_right)
+    def after(k):
+        pl.when(jnp.logical_and(odd_over, k == 2))(c_flr.start)
+
+        @pl.when(jnp.logical_and(odd_under, k == 2))
+        def _():
+            c_ulr.wait_recv()
+            c_ulf.start()
+
+    invert(s_ref, tile_ref, fac_ref, col_ref, ready, send_factor, after)
+
+    @pl.when(odd_over)
     def _():
         pack(ztiles.at[0])
-        for i in c_zl:
+        for i in c_zlr:
             i.start()
 
     store_inverse()
@@ -373,10 +388,23 @@
             fill_other(bufs.at[DO1])
             dout_ref[0] = cur[0]
 
-        invert(s_ref, tile_ref, fac_ref, col_ref, ready, lambda k: None)
+            @pl.when(odd_under)
+            def _():
+                for arriving, sent in zip(c_zlr, c_zl):
+                    arriving.wait_recv()
+                    sent.start()
+
+        def after(k):
+            @pl.when(jnp.logical_and(odd_under, k == 1))
+            def _():
+                c_flr.wait_recv()
+                c_flf[0].start()
+
+        invert(s_ref, tile_ref, fac_ref, col_ref, ready, lambda k: None, after)
         pack(ztiles.at[1])
         for i in c_za:
             i.start()
+        pl.when(odd_under)(c_flf[1].start)
         c_ru.wait_recv()
         c_rf.wait_recv()
 
@@ -390,21 +418,21 @@
         c_ru.start()
         c_uao.start()
         pl.when(even_right)(c_ul1.start)
-        cur[1] = u_ref[0]
-
-        @pl.when(has_left)
-        def _():
-            c_ul.wait_recv()
-            c_fl.wait_recv()
-            receive(ZL, ZLO, c_zl, c_zlo)
-            assemble(full_ref, u_ref.at[0], bufs.at[EO])
-            right(bufs.at[UL], bufs.at[FL], cur.at[0], cur.at[1], cur.at[2])
-
-        c_uo1.start()
         c_fb.wait_recv()
         fresh_ref[1] = bufs[FB] - dot3(scaled_ref[1], onward_ref[...])
         c_rf.start()
         pl.when(even_right)(c_fl1.start)
+        cur[1] = u_ref[0]
+
+        @pl.when(has_left)
+        def _():
+            receive(ZL, ZLO, c_zl, c_zlo)
+            assemble(full_ref, u_ref.at[0], bufs.at[EO])
+            ahead(ahead_ref)
+            c_ulf.wait_recv()
+            right(ahead_ref, bufs.at[UL], cur.at[0], cur.at[1])
+
+        c_uo1.start()
         c_uo1.wait_recv()
         assemble(full_ref, cur.at[1], bufs.at[UO1])
         uout_ref[0] = cur[1]
@@ -416,10 +444,15 @@
 
     @pl.when(even_left)
     def _():
+        receive(ZL1, ZL1O, c_zl1, c_zl1o)
+        ahead(onward_ref)
         c_ul1.wait_recv()
+        right(onward_ref, bufs.at[UL1], dout_ref.at[0], uout_ref.at[0])
         c_fl1.wait_recv()
-        receive(ZL1, ZL1O, c_zl1, c_zl1o)
-        right(bufs.at[UL1], bufs.at[FL1], dout_ref.at[0], uout_ref.at[0], fout_ref.at[0])
+        right_source(onward_ref, bufs.at[FL1], fout_ref.at[0])
+        for arriving, rows in zip(c_flf, (top, low)):
+            arriving.wait_recv()
+            right_source(ahead_ref, bufs.at[FL, rows], fout_ref.at[0, rows])
 
     def drained(condition, copies):
         @pl.when(condition)
@@ -429,7 +462,8 @@
 
     for i in (c_do, c_uo, c_eo):
         i.wait_send()
-    drained(odd_right, [c_ul, c_fl] + c_zl)
+    drained(odd_over, [c_ulr, c_flr] + c_zlr)
+    drained(odd_under, [c_ulf] + c_flf + c_zl)
     drained(even_left, c_zlo)
     drained(even, [copy_factor(k, c) for k in range(blocks) for c in range(k, blocks)])
     drained(odd, [c_e, c_fb, c_do1] + c_za)
@@ -438,10 +472,10 @@
     drained(even_left, c_zl1o)
 
 
-SLOTS = 15
-DO, UO, EO, EB, EX, UL, FL, FB, DO1, UO1, UAO, UL1, FL1, RU, RF = range(SLOTS)
-ZSLOTS = 6
-ZL, ZLO, ZA, ZAO, ZL1, ZL1O = range(ZSLOTS)
+SLOTS = 18
+DO, UO, EO, EB, EX, ULR, FLR, UL, FL, FB, DO1, UO1, UAO, UL1, FL1, FL2, RU, RF = range(SLOTS)
+ZSLOTS = 7
+ZLR, ZL, ZLO, ZA, ZAO, ZL1, ZL1O = range(ZSLOTS)
 ZTILES = 5
 
 
@@ -463,11 +497,12 @@
             pltpu.VMEM((size, size), F32),
             pltpu.VMEM((size, size), F32),
             pltpu.VMEM((size, size), F32),
+            pltpu.VMEM((size, size), F32),
             pltpu.VMEM((3, half, size), F32),
             pltpu.VMEM((2, half, size), F32),
             pltpu.VMEM((2, half, size), F32),
             pltpu.VMEM((2, ZTILES, tile, tile), F32),
-            pltpu.VMEM((RU, half, size), F32),
+            pltpu.VMEM((FL2, half, size), F32),
             pltpu.VMEM((ZSLOTS, ZTILES, tile, tile), F32),
             pltpu.VMEM((blocks, blocks, TILE, TILE), F32),
             pltpu.SemaphoreType.DMA((SLOTS,)),

time: 89.7 us -> 78.5 us (0.88)
  Pallas kernels: 86 us -> 74.5 us
    pallas_call x1, Pallas kernels: 86 us -> 74.5 us  [body(): pl.pallas_call(functools.partial(kernel, tm_size), out_shape=[jax.ShapeDt...]
where the time goes in v3:
time: 78.5 us; the launch traced here: 78 us
  Pallas kernels  74.5 us (95%)
  local copies, waits for them, and re-layouts  2.91 us (4%)
    pallas_call x1, Pallas kernels, body(): pl.pallas_call(functools.partial(kernel, tm_size), out_shape=[jax.ShapeDt...  74.5 us
    unnamed x3, local copies, waits for them, and re-layouts  2.91 us

profile of v3, /device:TPU:25, one launch (start us, length us, event | category | flops | bytes accessed | tf_op | source)
XLA Modules:
  0.0 78.0 jit_solution(16601521181993736297)
XLA Ops:
  0.6 74.5 %reduce_levels.1 = (f32[2,256,512]{2,1,0:T(8,128)S(1)}, f32[2,256,512]{2,1,0:T(8,128)S(1)}, f32[2,256,512]{2,1,0:T(8,128)S(1)}) custom-call(f32[2,256,512]{2,1,0:T(8,128)} %d_ref.1, f32[2,256,512]{2,1,0:T(8,128)} %u_ref.1, f32[2,256,512]{2,1,0:T(8,128)} %f_ref.1), custom_call_target="tpu_custom_call" | custom-call | tf_op jit(solution)/shard_map/reduce_levels/pallas_call | solution.py:487
  75.1 1.0 %copy.9 = f32[2,256,512]{2,1,0:T(8,128)} copy(f32[2,256,512]{2,1,0:T(8,128)S(1)} %get-tuple-element.6) | data formatting | bytes 2097152
  76.1 1.0 %copy.10 = f32[2,256,512]{2,1,0:T(8,128)} copy(f32[2,256,512]{2,1,0:T(8,128)S(1)} %get-tuple-element.7) | data formatting | bytes 2097152
  77.0 1.0 %copy.11 = f32[2,256,512]{2,1,0:T(8,128)} copy(f32[2,256,512]{2,1,0:T(8,128)S(1)} %get-tuple-element.8) | data formatting | bytes 2097152

commit v4 on v3

--- a/solution.py
+++ b/solution.py
@@ -307,6 +307,11 @@
     def right_source(product_ref, f, sto):
         sto[...] = sto[...] - dot3(f[...], product_ref[...])
 
+    def keep():
+        dout_ref[1] = d_ref[1]
+        uout_ref[1] = u_ref[1]
+        fout_ref[1] = f_ref[1]
+
     c_do = copy(DO, d_ref.at[1], "partner")
     c_uo = copy(UO, u_ref.at[1], "partner")
     c_eo = copy(EO, u_ref.at[0], "partner")
@@ -348,15 +353,16 @@
         c_do.wait_recv()
         fill_other(bufs.at[DO])
 
-    def after(k):
-        pl.when(jnp.logical_and(odd_over, k == 2))(c_flr.start)
-
-        @pl.when(jnp.logical_and(odd_under, k == 2))
+    def send(k):
+        send_factor(k)
+        pl.when(jnp.logical_and(odd_over, k == 1))(c_flr.start)
+
+        @pl.when(jnp.logical_and(odd_under, k == 1))
         def _():
             c_ulr.wait_recv()
             c_ulf.start()
 
-    invert(s_ref, tile_ref, fac_ref, col_ref, ready, send_factor, after)
+    invert(s_ref, tile_ref, fac_ref, col_ref, ready, send, lambda k: None)
 
     @pl.when(odd_over)
     def _():
@@ -370,9 +376,6 @@
         u_ref.at[1], bufs.at[UO], f_ref.at[1], d_ref.at[0], f_ref.at[0], cur.at[0], cur.at[2], scaled_ref
     )
     c_eo.wait_recv()
-    dout_ref[1] = d_ref[1]
-    uout_ref[1] = u_ref[1]
-    fout_ref[1] = f_ref[1]
 
     @pl.when(odd)
     def _():
@@ -402,9 +405,13 @@
 
         invert(s_ref, tile_ref, fac_ref, col_ref, ready, lambda k: None, after)
         pack(ztiles.at[1])
-        for i in c_za:
+        for n, i in enumerate(c_za):
             i.start()
+            if n > 0:
+                c_za[n - 1].wait_send()
+        c_za[-1].wait_send()
         pl.when(odd_under)(c_flf[1].start)
+        keep()
         c_ru.wait_recv()
         c_rf.wait_recv()
 
@@ -433,10 +440,17 @@
             right(ahead_ref, bufs.at[UL], cur.at[0], cur.at[1])
 
         c_uo1.start()
+        keep()
         c_uo1.wait_recv()
         assemble(full_ref, cur.at[1], bufs.at[UO1])
         uout_ref[0] = cur[1]
         c_uao.wait_recv()
+
+        @pl.when(has_left)
+        def _():
+            c_flf[0].wait_recv()
+            right_source(ahead_ref, bufs.at[FL, top], cur.at[2, top])
+
         receive(ZA, ZAO, c_za, c_zao, c_zl1, even_right)
         left(
             fresh_ref.at[0], bufs.at[UAO], fresh_ref.at[1], cur.at[0], cur.at[2], dout_ref.at[0], fout_ref.at[0]
@@ -450,9 +464,8 @@
         right(onward_ref, bufs.at[UL1], dout_ref.at[0], uout_ref.at[0])
         c_fl1.wait_recv()
         right_source(onward_ref, bufs.at[FL1], fout_ref.at[0])
-        for arriving, rows in zip(c_flf, (top, low)):
-            arriving.wait_recv()
-            right_source(ahead_ref, bufs.at[FL, rows], fout_ref.at[0, rows])
+        c_flf[1].wait_recv()
+        right_source(ahead_ref, bufs.at[FL, low], fout_ref.at[0, low])
 
     def drained(condition, copies):
         @pl.when(condition)
@@ -466,7 +479,7 @@
     drained(odd_under, [c_ulf] + c_flf + c_zl)
     drained(even_left, c_zlo)
     drained(even, [copy_factor(k, c) for k in range(blocks) for c in range(k, blocks)])
-    drained(odd, [c_e, c_fb, c_do1] + c_za)
+    drained(odd, [c_e, c_fb, c_do1])
     drained(even, [c_ex, c_ru, c_rf, c_uao, c_uo1] + c_zao)
     drained(even_right, [c_ul1, c_fl1] + c_zl1)
     drained(even_left, c_zl1o)

time: 78.5 us -> 76.5 us (0.975)
  Pallas kernels: 74.5 us -> 72.4 us
    pallas_call x1, Pallas kernels: 74.5 us -> 72.4 us  [body(): pl.pallas_call(functools.partial(kernel, tm_size), out_shape=[jax.ShapeDt...]
where the time goes in v4:
time: 76.5 us; the launch traced here: 75.9 us
  Pallas kernels  72.4 us (95%)
  local copies, waits for them, and re-layouts  2.91 us (4%)
    pallas_call x1, Pallas kernels, body(): pl.pallas_call(functools.partial(kernel, tm_size), out_shape=[jax.ShapeDt...  72.4 us
    unnamed x3, local copies, waits for them, and re-layouts  2.91 us

profile of v4, /device:TPU:25, one launch (start us, length us, event | category | flops | bytes accessed | tf_op | source)
XLA Modules:
  0.0 75.9 jit_solution(13645797736790913778)
XLA Ops:
  0.6 72.4 %reduce_levels.1 = (f32[2,256,512]{2,1,0:T(8,128)S(1)}, f32[2,256,512]{2,1,0:T(8,128)S(1)}, f32[2,256,512]{2,1,0:T(8,128)S(1)}) custom-call(f32[2,256,512]{2,1,0:T(8,128)} %d_ref.1, f32[2,256,512]{2,1,0:T(8,128)} %u_ref.1, f32[2,256,512]{2,1,0:T(8,128)} %f_ref.1), custom_call_target="tpu_custom_call" | custom-call | tf_op jit(solution)/shard_map/reduce_levels/pallas_call | solution.py:500
  73.0 1.0 %copy.9 = f32[2,256,512]{2,1,0:T(8,128)} copy(f32[2,256,512]{2,1,0:T(8,128)S(1)} %get-tuple-element.6) | data formatting | bytes 2097152
  74.0 1.0 %copy.10 = f32[2,256,512]{2,1,0:T(8,128)} copy(f32[2,256,512]{2,1,0:T(8,128)S(1)} %get-tuple-element.7) | data formatting | bytes 2097152
  75.0 1.0 %copy.11 = f32[2,256,512]{2,1,0:T(8,128)} copy(f32[2,256,512]{2,1,0:T(8,128)S(1)} %get-tuple-element.8) | data formatting | bytes 2097152

commit v5 on v4

--- a/solution.py
+++ b/solution.py
@@ -198,10 +198,13 @@
             device_id=targets[target], device_id_type=pl.DeviceIdType.MESH,
         )
 
+    def extent(i):
+        return slice(0, tile + PANEL if i == 0 else tile)
+
     def copy_tiles(slot, source, target):
         return [
             pltpu.make_async_remote_copy(
-                src_ref=source.at[i], dst_ref=zbufs.at[slot, i],
+                src_ref=source.at[i, extent(i)], dst_ref=zbufs.at[slot, i, extent(i)],
                 send_sem=zsend_sem.at[ZTILES * slot + i], recv_sem=zrecv_sem.at[ZTILES * slot + i],
                 device_id=targets[target], device_id_type=pl.DeviceIdType.MESH,
             )
@@ -218,15 +221,21 @@
 
         first, far = c * half, (1 - c) * half
         near = [at(first), at(first + tile)]
-        return [
-            (near[0], near[0]), (near[0], near[1]), (near[1], near[1]),
-            (near[0], at(far + c * tile)), (near[1], at(far + (1 - c) * tile)),
+        return near, [
+            (near[0], near[1]), (near[0], at(far + c * tile)), (near[1], at(far + (1 - c) * tile)),
         ]
 
+    down = lax.broadcasted_iota(jnp.int32, (tile, tile), 0)
+    across = lax.broadcasted_iota(jnp.int32, (tile, tile), 1)
+
     def pack(into):
-        places = [(0, 0), (0, tile), (tile, tile), (0, half + column * tile), (tile, half + partner * tile)]
+        first, second = s_ref[:tile, :tile], s_ref[tile:half, tile:half]
+        into[0, :tile] = jnp.where(down > across, first, second)
+        middle = jnp.sum(jnp.where(down == across, first, 0.0), axis=0, keepdims=True)
+        into[0, tile:] = jnp.broadcast_to(middle, (PANEL, tile))
+        places = [(0, tile), (0, half + column * tile), (tile, half + partner * tile)]
         for i, (row, col) in enumerate(places):
-            into[i] = s_ref[row : row + tile, pl.ds(pl.multiple_of(col, tile), tile)]
+            into[1 + i, :tile] = s_ref[row : row + tile, pl.ds(pl.multiple_of(col, tile), tile)]
 
     def fill_own(source):
         s_ref[:half, :half] = source[:, own_at]
@@ -257,11 +266,18 @@
             pl.when(jnp.logical_and(even, c >= k))(copy_factor(k, c).start)
 
     def unpack(slot, c):
-        for i, (row, col) in enumerate(tile_places(c)):
-            value = zbufs[slot, i]
+        near, places = tile_places(c)
+        both = zbufs[slot, 0, :tile]
+        turned = both.T
+        middle = jnp.broadcast_to(zbufs[slot, 0, tile : tile + 1], (tile, tile))
+        z_ref[near[0], near[0]] = jnp.where(
+            down > across, both, jnp.where(down < across, turned, middle)
+        )
+        z_ref[near[1], near[1]] = jnp.where(down > across, turned, both)
+        for i, (row, col) in enumerate(places):
+            value = zbufs[slot, 1 + i, :tile]
             z_ref[row, col] = value
-            if i not in (0, 2):
-                z_ref[col, row] = value.T
+            z_ref[col, row] = value.T
 
     def receive(slot, other_slot, arriving, shared, onward=None, condition=None):
         for i in range(ZTILES):
@@ -489,7 +505,7 @@
 DO, UO, EO, EB, EX, ULR, FLR, UL, FL, FB, DO1, UO1, UAO, UL1, FL1, FL2, RU, RF = range(SLOTS)
 ZSLOTS = 7
 ZLR, ZL, ZLO, ZA, ZAO, ZL1, ZL1O = range(ZSLOTS)
-ZTILES = 5
+ZTILES = 4
 
 
 def body(tm_size, diagonal_blocks, upper_blocks, right_sides):
@@ -514,9 +530,9 @@
             pltpu.VMEM((3, half, size), F32),
             pltpu.VMEM((2, half, size), F32),
             pltpu.VMEM((2, half, size), F32),
-            pltpu.VMEM((2, ZTILES, tile, tile), F32),
+            pltpu.VMEM((2, ZTILES, tile + PANEL, tile), F32),
             pltpu.VMEM((FL2, half, size), F32),
-            pltpu.VMEM((ZSLOTS, ZTILES, tile, tile), F32),
+            pltpu.VMEM((ZSLOTS, ZTILES, tile + PANEL, tile), F32),
             pltpu.VMEM((blocks, blocks, TILE, TILE), F32),
             pltpu.SemaphoreType.DMA((SLOTS,)),
             pltpu.SemaphoreType.DMA((SLOTS,)),

time: 76.5 us -> 73.2 us (0.957)
  Pallas kernels: 72.4 us -> 69.1 us
    pallas_call x1, Pallas kernels: 72.4 us -> 69.1 us  [body(): pl.pallas_call(functools.partial(kernel, tm_size), out_shape=[jax.ShapeDt...]
where the time goes in v5:
time: 73.2 us; the launch traced here: 72.7 us
  Pallas kernels  69.1 us (94%)
  local copies, waits for them, and re-layouts  2.91 us (4%)
    pallas_call x1, Pallas kernels, body(): pl.pallas_call(functools.partial(kernel, tm_size), out_shape=[jax.ShapeDt...  69.1 us
    unnamed x3, local copies, waits for them, and re-layouts  2.91 us

profile of v5, /device:TPU:25, one launch (start us, length us, event | category | flops | bytes accessed | tf_op | source)
XLA Modules:
  0.0 72.7 jit_solution(17901541981587204043)
XLA Ops:
  0.6 69.1 %reduce_levels.1 = (f32[2,256,512]{2,1,0:T(8,128)S(1)}, f32[2,256,512]{2,1,0:T(8,128)S(1)}, f32[2,256,512]{2,1,0:T(8,128)S(1)}) custom-call(f32[2,256,512]{2,1,0:T(8,128)} %d_ref.1, f32[2,256,512]{2,1,0:T(8,128)} %u_ref.1, f32[2,256,512]{2,1,0:T(8,128)} %f_ref.1), custom_call_target="tpu_custom_call" | custom-call | tf_op jit(solution)/shard_map/reduce_levels/pallas_call | solution.py:516
  69.7 1.0 %copy.9 = f32[2,256,512]{2,1,0:T(8,128)} copy(f32[2,256,512]{2,1,0:T(8,128)S(1)} %get-tuple-element.6) | data formatting | bytes 2097152
  70.7 1.0 %copy.10 = f32[2,256,512]{2,1,0:T(8,128)} copy(f32[2,256,512]{2,1,0:T(8,128)S(1)} %get-tuple-element.7) | data formatting | bytes 2097152
  71.7 1.0 %copy.11 = f32[2,256,512]{2,1,0:T(8,128)} copy(f32[2,256,512]{2,1,0:T(8,128)S(1)} %get-tuple-element.8) | data formatting | bytes 2097152
